TPU v7x, 32 devices: a whole 2x2x4 slice. The times are simulated.
32 devices in a mesh: dp: 8 (over z, x), shard: 4 (over y, core).
Axes of the slice: x: 2, y: 2, z: 4, core: 2. Of those that a mesh axis runs over, the one named last changes fastest.
Arguments:
- target: bfloat16 [32, 1024, 512], P(('dp', 'shard')), may hold values from -6 to 6
- memory: bfloat16 [32, 1024, 512], P(('dp', 'shard')), may hold values from -6 to 6
- cotangent: bfloat16 [32, 1024, 512], P(('dp', 'shard')), may hold values from -6 to 6
- target_lengths: int32 [32, 24], P(('dp', 'shard')), may hold values from 1 to 512, 1024 in all within a row
- source_lengths: int32 [32, 24], P(('dp', 'shard')), may hold values from 1 to 512, 1024 in all within a row
- inward_master: float32 [1572864], P(('dp', 'shard')), may hold values from -0.25 to 0.25
- inward_mean: float32 [1572864], P(('dp', 'shard')), may hold values from -320 to 320
- inward_square: float32 [1572864], P(('dp', 'shard')), may hold values from 327.68 to 32768
- outward_master: float32 [524288], P(('dp', 'shard')), may hold values from -0.75 to 0.75
- outward_mean: float32 [524288], P(('dp', 'shard')), may hold values from -320 to 320
- outward_square: float32 [524288], P(('dp', 'shard')), may hold values from 327.68 to 32768
- expand_master: float32 [1048576], P(('dp', 'shard')), may hold values from -0.25 to 0.25
- expand_mean: float32 [1048576], P(('dp', 'shard')), may hold values from -320 to 320
- expand_square: float32 [1048576], P(('dp', 'shard')), may hold values from 327.68 to 32768
- shrink_master: float32 [1048576], P(('dp', 'shard')), may hold values from -0.125 to 0.125
- shrink_mean: float32 [1048576], P(('dp', 'shard')), may hold values from -320 to 320
- shrink_square: float32 [1048576], P(('dp', 'shard')), may hold values from 327.68 to 32768
- norms_master: float32 [3072], P(('dp', 'shard')), may hold values from -0.5 to 1.3, as said below
- norms_mean: float32 [3072], P(('dp', 'shard')), may hold values from -320 to 320
- norms_square: float32 [3072], P(('dp', 'shard')), may hold values from 327.68 to 32768
Outputs:
- result: bfloat16 [32, 1024, 512], P(('dp', 'shard'))
- target_grad: float32 [32, 1024, 512], P(('dp', 'shard'))
- memory_grad: float32 [32, 1024, 512], P(('dp', 'shard'))
- change_inward: float32 [1572864], P(('dp', 'shard'))
- mean_inward: float32 [1572864], P(('dp', 'shard'))
- summed_inward: float32 [1572864], P(('dp', 'shard'))
- change_outward: float32 [524288], P(('dp', 'shard'))
- mean_outward: float32 [524288], P(('dp', 'shard'))
- summed_outward: float32 [524288], P(('dp', 'shard'))
- change_expand: float32 [1048576], P(('dp', 'shard'))
- mean_expand: float32 [1048576], P(('dp', 'shard'))
- summed_expand: float32 [1048576], P(('dp', 'shard'))
- change_shrink: float32 [1048576], P(('dp', 'shard'))
- mean_shrink: float32 [1048576], P(('dp', 'shard'))
- summed_shrink: float32 [1048576], P(('dp', 'shard'))
- change_norms: float32 [3072], P(('dp', 'shard'))
- mean_norms: float32 [3072], P(('dp', 'shard'))
- summed_norms: float32 [3072], P(('dp', 'shard'))
Inputs may be any that keep to these rules, and one draw needn't show every extreme that they name: `target_lengths`: in each row the 24 lengths sum to 1024; the last entry is padding, the others are sentences; target sentence i is the translation of source sentence i. `source_lengths`: as target_lengths, for the source side. `norms_master`: the first 1536 entries are gains, the others biases.
All inputs are finite; a program needn't handle non-finite values.
Results may differ from a plain program's by a relative error of at most 0.015.
The roundings to bfloat16 on the way count: a program that leaves them out, or rounds other values in their place, can miss the bound.
Values may be sent and summed in bfloat16 or wider, within the bound.
A program may use at most 192 MiB of HBM per device.

v0:
```python
import jax
import jax.numpy as jnp
from jax import lax
from jax.sharding import PartitionSpec as P

D = 512
HEADS = 8
HD = 64
FF = 2048
ROW = 1024
SEGS = 24
STEP = 10
learn_rate = 0.001
beta_one = 0.9
beta_two = 0.999


def matmul(left_mat, right_mat):
    return jnp.dot(left_mat, right_mat, preferred_element_type=jnp.float32)


def left_dot(left_mat, right_mat):
    return lax.dot_general(
        left_mat, right_mat, (((0,), (0,)), ((), ())), preferred_element_type=jnp.float32
    )


def right_dot(left_mat, right_mat):
    return lax.dot_general(
        left_mat, right_mat, (((1,), (1,)), ((), ())), preferred_element_type=jnp.float32
    )


def layer_norm(residual, norm_gain, norm_bias):
    centered = residual - jnp.mean(residual, -1, keepdims=True)
    spread = jnp.mean(centered * centered, -1, keepdims=True)
    return centered * lax.rsqrt(spread + 1e-05) * norm_gain + norm_bias


def segments(lengths):
    ends = jnp.cumsum(lengths, axis=-1)
    places = jnp.arange(ROW, dtype=jnp.int32)
    return jnp.sum((places[None, :, None] >= ends[:, None, :]).astype(jnp.int32), -1)


def pair_mask(query_seg, key_seg, row_start, causal):
    allowed = query_seg[:, None] == key_seg[None, :]
    if causal:
        query_pos = row_start + jnp.arange(query_seg.shape[0], dtype=jnp.int32)
        key_pos = jnp.arange(key_seg.shape[0], dtype=jnp.int32)
        allowed = allowed & (key_pos[None, :] <= query_pos[:, None])
    return allowed


def attend(queries, keys, values, query_seg, key_seg, causal):
    block_rows = min(512, queries.shape[1])
    block_count = queries.shape[1] // block_rows
    score_scale = queries.shape[3] ** (-0.5)

    def one_row(row_items):
        q_row, k_row, v_row, qs_row, ks_row = row_items

        def one_block(block_index):
            row_start = block_index * block_rows
            q_block = lax.dynamic_slice_in_dim(q_row, row_start, block_rows, 0)
            seg_block = lax.dynamic_slice_in_dim(qs_row, row_start, block_rows, 0)
            scores = (
                jnp.einsum("qhd,khd->hqk", q_block, k_row, preferred_element_type=jnp.float32)
                * score_scale
            )
            allowed = pair_mask(seg_block, ks_row, row_start, causal)
            scores = jnp.where(allowed[None], scores, -1000000000.0)
            row_peak = jnp.max(scores, -1, keepdims=True)
            raised = jnp.exp(scores - row_peak)
            row_total = jnp.sum(raised, -1, keepdims=True)
            probs = (raised / row_total).astype(jnp.bfloat16)
            context = jnp.einsum("hqk,khd->qhd", probs, v_row, preferred_element_type=jnp.float32)
            return (context, row_peak[..., 0] + jnp.log(row_total[..., 0]))

        context, logsum = lax.map(one_block, jnp.arange(block_count, dtype=jnp.int32))
        return (context.reshape(-1, q_row.shape[1] * q_row.shape[2]), logsum)

    return lax.map(one_row, (queries, keys, values, query_seg, key_seg))


def attend_back(queries, keys, values, logsum, grad_ctx, query_seg, key_seg, causal):
    block_rows = min(512, queries.shape[1])
    block_count = queries.shape[1] // block_rows
    score_scale = queries.shape[3] ** (-0.5)

    def one_row(row_items):
        q_row, k_row, v_row, ls_row, g_row, qs_row, ks_row = row_items

        def one_block(carry, block_index):
            grad_keys, grad_values = carry
            row_start = block_index * block_rows
            q_block = lax.dynamic_slice_in_dim(q_row, row_start, block_rows, 0)
            g_block = lax.dynamic_slice_in_dim(g_row, row_start, block_rows, 0)
            seg_block = lax.dynamic_slice_in_dim(qs_row, row_start, block_rows, 0)
            ls_block = lax.dynamic_index_in_dim(ls_row, block_index, 0, keepdims=False)
            scores = (
                jnp.einsum("qhd,khd->hqk", q_block, k_row, preferred_element_type=jnp.float32)
                * score_scale
            )
            allowed = pair_mask(seg_block, ks_row, row_start, causal)
            probs = jnp.where(allowed[None], jnp.exp(scores - ls_block[..., None]), 0.0)
            grad_probs = jnp.einsum(
                "qhd,khd->hqk", g_block, v_row, preferred_element_type=jnp.float32
            )
            inner = jnp.sum(probs * grad_probs, -1, keepdims=True)
            grad_scores = (probs * (grad_probs - inner) * score_scale).astype(jnp.bfloat16)
            grad_query = jnp.einsum(
                "hqk,khd->qhd", grad_scores, k_row, preferred_element_type=jnp.float32
            )
            grad_keys = grad_keys + jnp.einsum(
                "hqk,qhd->khd", grad_scores, q_block, preferred_element_type=jnp.float32
            )
            grad_values = grad_values + jnp.einsum(
                "hqk,qhd->khd",
                probs.astype(jnp.bfloat16),
                g_block,
                preferred_element_type=jnp.float32,
            )
            return ((grad_keys, grad_values), grad_query)

        empty = jnp.zeros(k_row.shape, jnp.float32)
        (grad_keys, grad_values), grad_query = lax.scan(
            one_block, (empty, empty), jnp.arange(block_count, dtype=jnp.int32)
        )
        return (grad_query.reshape(q_row.shape), grad_keys, grad_values)

    return lax.map(one_row, (queries, keys, values, logsum, grad_ctx, query_seg, key_seg))


def unpack(inward_all, outward_all, norms_all, expand_all, shrink_all):
    norm_par = norms_all.reshape(2, 3, D).astype(jnp.float32)
    return (
        inward_all.reshape(6, D, D),
        outward_all.reshape(2, D, D),
        expand_all.reshape(D, FF),
        shrink_all.reshape(FF, D),
        norm_par[0],
        norm_par[1],
    )


def adam_step(mean_old, square_old, grad_share):
    mean_new = beta_one * mean_old + (1.0 - beta_one) * grad_share
    square_new = beta_two * square_old + (1.0 - beta_two) * grad_share * grad_share
    steps_float = float(STEP)
    mean_hat = mean_new / (1.0 - beta_one**steps_float)
    square_hat = square_new / (1.0 - beta_two**steps_float)
    change = -learn_rate * mean_hat / (jnp.sqrt(square_hat) + 1e-08)
    return (change, mean_new, grad_share)


def body(
    target,
    memory,
    cotangent,
    target_lengths,
    source_lengths,
    inward_master,
    inward_mean,
    inward_square,
    outward_master,
    outward_mean,
    outward_square,
    expand_master,
    expand_mean,
    expand_square,
    shrink_master,
    shrink_mean,
    shrink_square,
    norms_master,
    norms_mean,
    norms_square,
):
    row_count = target.shape[0]
    inward_low = inward_master.astype(jnp.bfloat16)
    outward_low = outward_master.astype(jnp.bfloat16)
    expand_low = expand_master.astype(jnp.bfloat16)
    shrink_low = shrink_master.astype(jnp.bfloat16)
    norms_low = norms_master.astype(jnp.bfloat16)
    inward_all, outward_all, norms_all = (
        lax.all_gather(inward_low, ("dp", "shard"), axis=0, tiled=True),
        lax.all_gather(outward_low, ("dp", "shard"), axis=0, tiled=True),
        lax.all_gather(norms_low, ("dp", "shard"), axis=0, tiled=True),
    )
    expand_all, shrink_all = (
        lax.all_gather(expand_low, ("dp", "shard"), axis=0, tiled=True),
        lax.all_gather(shrink_low, ("dp", "shard"), axis=0, tiled=True),
    )
    w_in, w_out, w_up, w_down, gains, biases = unpack(
        inward_all, outward_all, norms_all, expand_all, shrink_all
    )
    target_seg = segments(target_lengths)
    source_seg = segments(source_lengths)
    live_rows = (target_seg < SEGS - 1).astype(jnp.float32).reshape(-1, 1)

    def heads(values_flat):
        return values_flat.reshape(row_count, ROW, HEADS, HD)

    tokens = target.reshape(-1, D)
    source = memory.reshape(-1, D)
    query_one = matmul(tokens, w_in[0]).astype(jnp.bfloat16)
    key_one = matmul(tokens, w_in[1]).astype(jnp.bfloat16)
    value_one = matmul(tokens, w_in[2]).astype(jnp.bfloat16)
    ctx_raw, logsum_one = attend(
        heads(query_one), heads(key_one), heads(value_one), target_seg, target_seg, True
    )
    ctx_one = ctx_raw.reshape(-1, D).astype(jnp.bfloat16)
    resid_one = tokens.astype(jnp.float32) + matmul(ctx_one, w_out[0])
    hidden_one = layer_norm(resid_one, gains[0], biases[0])
    hidden_low = hidden_one.astype(jnp.bfloat16)
    query_two = matmul(hidden_low, w_in[3]).astype(jnp.bfloat16)
    key_two = matmul(source, w_in[4]).astype(jnp.bfloat16)
    value_two = matmul(source, w_in[5]).astype(jnp.bfloat16)
    ctx_raw, logsum_two = attend(
        heads(query_two), heads(key_two), heads(value_two), target_seg, source_seg, False
    )
    ctx_two = ctx_raw.reshape(-1, D).astype(jnp.bfloat16)
    resid_two = hidden_one + matmul(ctx_two, w_out[1])
    hidden_two = layer_norm(resid_two, gains[1], biases[1])
    second_low = hidden_two.astype(jnp.bfloat16)
    pre_act = matmul(second_low, w_up)
    activated = jax.nn.silu(pre_act).astype(jnp.bfloat16)
    resid_three = hidden_two + matmul(activated, w_down)
    output = layer_norm(resid_three, gains[2], biases[2])
    inward_back, outward_back, norms_back, expand_back, shrink_back = (
        lax.all_gather(inward_low, ("dp", "shard"), axis=0, tiled=True),
        lax.all_gather(outward_low, ("dp", "shard"), axis=0, tiled=True),
        lax.all_gather(norms_low, ("dp", "shard"), axis=0, tiled=True),
        lax.all_gather(expand_low, ("dp", "shard"), axis=0, tiled=True),
        lax.all_gather(shrink_low, ("dp", "shard"), axis=0, tiled=True),
    )
    w_in, w_out, w_up, w_down, gains, biases = unpack(
        inward_back, outward_back, norms_back, expand_back, shrink_back
    )
    seed = cotangent.reshape(-1, D).astype(jnp.float32) * live_rows
    _, pull_three = jax.vjp(layer_norm, resid_three, gains[2], biases[2])
    grad_three, gain_three, bias_three = pull_three(seed)
    grad_out = grad_three.astype(jnp.bfloat16)
    grad_shrink = left_dot(activated, grad_out)
    grad_act = right_dot(grad_out, w_down)
    _, pull_act = jax.vjp(jax.nn.silu, pre_act)
    grad_pre = pull_act(grad_act)[0].astype(jnp.bfloat16)
    grad_expand = left_dot(second_low, grad_pre)
    grad_hidden_two = grad_three + right_dot(grad_pre, w_up)
    _, pull_two = jax.vjp(layer_norm, resid_two, gains[1], biases[1])
    grad_two, gain_two, bias_two = pull_two(grad_hidden_two)
    branch_two = grad_two.astype(jnp.bfloat16)
    grad_wo_two = left_dot(ctx_two, branch_two)
    grad_ctx_two = right_dot(branch_two, w_out[1]).astype(jnp.bfloat16)
    dq_two, dk_two, dv_two = attend_back(
        heads(query_two),
        heads(key_two),
        heads(value_two),
        logsum_two,
        heads(grad_ctx_two),
        target_seg,
        source_seg,
        False,
    )
    dq_two = dq_two.reshape(-1, D).astype(jnp.bfloat16)
    dk_two = dk_two.reshape(-1, D).astype(jnp.bfloat16)
    dv_two = dv_two.reshape(-1, D).astype(jnp.bfloat16)
    grad_wq_two = left_dot(hidden_low, dq_two)
    grad_wk_two = left_dot(source, dk_two)
    grad_wv_two = left_dot(source, dv_two)
    memory_grad = right_dot(dk_two, w_in[4]) + right_dot(dv_two, w_in[5])
    grad_hidden_one = grad_two + right_dot(dq_two, w_in[3])
    _, pull_one = jax.vjp(layer_norm, resid_one, gains[0], biases[0])
    grad_one, gain_one, bias_one = pull_one(grad_hidden_one)
    branch_one = grad_one.astype(jnp.bfloat16)
    grad_wo_one = left_dot(ctx_one, branch_one)
    grad_ctx_one = right_dot(branch_one, w_out[0]).astype(jnp.bfloat16)
    dq_one, dk_one, dv_one = attend_back(
        heads(query_one),
        heads(key_one),
        heads(value_one),
        logsum_one,
        heads(grad_ctx_one),
        target_seg,
        target_seg,
        True,
    )
    dq_one = dq_one.reshape(-1, D).astype(jnp.bfloat16)
    dk_one = dk_one.reshape(-1, D).astype(jnp.bfloat16)
    dv_one = dv_one.reshape(-1, D).astype(jnp.bfloat16)
    grad_wq_one = left_dot(tokens, dq_one)
    grad_wk_one = left_dot(tokens, dk_one)
    grad_wv_one = left_dot(tokens, dv_one)
    target_grad = (
        grad_one
        + right_dot(dq_one, w_in[0])
        + right_dot(dk_one, w_in[1])
        + right_dot(dv_one, w_in[2])
    )
    grad_inward = jnp.stack(
        [grad_wq_one, grad_wk_one, grad_wv_one, grad_wq_two, grad_wk_two, grad_wv_two]
    ).reshape(-1)
    grad_outward = jnp.stack([grad_wo_one, grad_wo_two]).reshape(-1)
    grad_norms = jnp.stack(
        [jnp.stack([gain_one, gain_two, gain_three]), jnp.stack([bias_one, bias_two, bias_three])]
    ).reshape(-1)
    inward_share, outward_share, norms_share, expand_share, shrink_share = (
        lax.psum_scatter(grad_inward, ("dp", "shard"), scatter_dimension=0, tiled=True),
        lax.psum_scatter(grad_outward, ("dp", "shard"), scatter_dimension=0, tiled=True),
        lax.psum_scatter(grad_norms, ("dp", "shard"), scatter_dimension=0, tiled=True),
        lax.psum_scatter(grad_expand.reshape(-1), ("dp", "shard"), scatter_dimension=0, tiled=True),
        lax.psum_scatter(grad_shrink.reshape(-1), ("dp", "shard"), scatter_dimension=0, tiled=True),
    )
    in_c, in_m, in_g = adam_step(inward_mean, inward_square, inward_share)
    out_c, out_m, out_g = adam_step(outward_mean, outward_square, outward_share)
    up_c, up_m, up_g = adam_step(expand_mean, expand_square, expand_share)
    down_c, down_m, down_g = adam_step(shrink_mean, shrink_square, shrink_share)
    norm_c, norm_m, norm_g = adam_step(norms_mean, norms_square, norms_share)
    shape_rows = (row_count, ROW, D)
    return (
        output.astype(jnp.bfloat16).reshape(shape_rows),
        target_grad.reshape(shape_rows),
        memory_grad.reshape(shape_rows),
        in_c,
        in_m,
        in_g,
        out_c,
        out_m,
        out_g,
        up_c,
        up_m,
        up_g,
        down_c,
        down_m,
        down_g,
        norm_c,
        norm_m,
        norm_g,
    )


def solution(mesh):
    return jax.shard_map(
        body,
        mesh=mesh,
        in_specs=(
            P(("dp", "shard"), None, None),
            P(("dp", "shard"), None, None),
            P(("dp", "shard"), None, None),
            P(("dp", "shard"), None),
            P(("dp", "shard"), None),
            P(("dp", "shard")),
            P(("dp", "shard")),
            P(("dp", "shard")),
            P(("dp", "shard")),
            P(("dp", "shard")),
            P(("dp", "shard")),
            P(("dp", "shard")),
            P(("dp", "shard")),
            P(("dp", "shard")),
            P(("dp", "shard")),
            P(("dp", "shard")),
            P(("dp", "shard")),
            P(("dp", "shard")),
            P(("dp", "shard")),
            P(("dp", "shard")),
        ),
        out_specs=(
            P(("dp", "shard"), None, None),
            P(("dp", "shard"), None, None),
            P(("dp", "shard"), None, None),
            P(("dp", "shard")),
            P(("dp", "shard")),
            P(("dp", "shard")),
            P(("dp", "shard")),
            P(("dp", "shard")),
            P(("dp", "shard")),
            P(("dp", "shard")),
            P(("dp", "shard")),
            P(("dp", "shard")),
            P(("dp", "shard")),
            P(("dp", "shard")),
            P(("dp", "shard")),
            P(("dp", "shard")),
            P(("dp", "shard")),
            P(("dp", "shard")),
        ),
        check_vma=False,
    )
```

profile of v0, /device:TPU:0, one launch (start us, length us, event | category | flops | bytes accessed | tf_op | source)
XLA Modules:
  0.0 1016.5 jit_solution(18071916766514258898)
XLA Ops:
  17.8 42.1 %all-reduce = bf16[3072]{0:T(1024)(128)(2,1)S(1)} all-reduce(bf16[3072]{0:T(1024)(128)(2,1)S(1)} %dynamic-update-slice), channel_id=1, replica_groups=mesh['dp'=8,'shard'=4] {'dp','shard'}, use_global_device_ids=true, to_apply=%add | all-reduce | flops 3072 | bytes 12288
  71.8 55.1 %all-gather.9.cloned.1.call-done = bf16[1048576]{0:T(1024)(128)(2,1)} async-done(((bf16[32768]{0:T(1024)(128)(2,1)}), bf16[1048576]{0:T(1024)(128)(2,1)}) %all-gather.9.cloned.1.call-update) | async-done | bytes 2097168 | tf_op jit(solution)/shard_map/all_gather | solution.py:191
  131.1 54.6 %all-gather.11.cloned.1.call-done = bf16[1048576]{0:T(1024)(128)(2,1)} async-done(((bf16[32768]{0:T(1024)(128)(2,1)}), bf16[1048576]{0:T(1024)(128)(2,1)}) %all-gather.11.cloned.1.call-update) | async-done | bytes 2097168 | tf_op jit(solution)/shard_map/all_gather | solution.py:192
  190.0 56.9 %all-gather.5.cloned.1.call-done = bf16[1572864]{0:T(1024)(128)(2,1)} async-done(((bf16[49152]{0:T(1024)(128)(2,1)}), bf16[1572864]{0:T(1024)(128)(2,1)}) %all-gather.5.cloned.1.call-update) | async-done | bytes 3145744 | tf_op jit(solution)/shard_map/all_gather | solution.py:186
  267.0 33.5 %while.96 = (s32[]{:T(128)}, bf16[2,512,8,64]{1,3,2,0:T(8,128)(2,1)}, f32[2,8,512]{2,1,0:T(8,128)S(1)}, s32[2]{0:T(128)S(1)}, s32[1024]{0:T(1024)S(1)}, /*index=...) while((s32[]{:T(128)}, ...), condition=%wide.region_5.6_spmd, body=%wide.region_2.0_spmd.sunk | while | flops 1125642752 | bytes 64633092 | solution.py:80
  309.4 41.3 %while.97 = (s32[]{:T(128)}, bf16[2,512,8,64]{1,3,2,0:T(8,128)(2,1)}, f32[2,8,512]{2,1,0:T(8,128)S(1)}, s32[2]{0:T(128)S(1)}, s32[1024]{0:T(1024)S(1)}, /*index=...) while((s32[]{:T(128)}, ...), condition=%wide.region_13.14_spmd, body=%wide.region_10.13_spmd.sunk | while | flops 1124593664 | bytes 64628996 | solution.py:80
  389.0 141.6 %while.98 = (s32[]{:T(128)}, f32[1024,8,64]{0,2,1:T(8,128)}, f32[1024,8,64]{0,2,1:T(8,128)}, bf16[2,512,8,64]{1,3,2,0:T(8,128)(2,1)}, s32[2]{0:T(128)S(1)}, /*in...) while((s32[]{:T(128)}, f32[1024,8,64]{0,2,1:T(8,128)}, ...), condition=%wide.region_24.25_spmd.clone, body=%wide.region_22.24_spmd.clone.sunk | while | flops 2745706496 | bytes 267446608 | solution.py:127
  405.2 8.1 fusion.275
  413.3 22.7 %fusion.276 = bf16[2,512,8,64]{1,3,2,0:T(8,128)(2,1)} fusion(bf16[2,512,8,64]{1,3,2,0:T(8,128)(2,1)} %get-tuple-element.1065, s32[]{:T(128)S(6)} %copy.136, bf16[1024,8,64]{0,2,1:T(8,128)(2,1)} %get-tuple-element.1087, f32[8,512,1024]{2,1,0:T(8,128)} %copy-done.1, f32[8,512,1024]{2,1,0:T(8,128)} %fusion.275), kind=kOutput, calls=%fused_computation.46.clone.1 | convolution fusion | flops 557847552 | bytes 69206016 | tf_op jit(solution)/shard_map/while/body/eval_jaxpr/while/body/eval_jaxpr/hqk,khd->qhd/dot_general | solution.py:112
  436.0 23.4 %bitcast_add_fusion.8 = f32[1024,8,64]{0,2,1:T(8,128)} fusion(f32[1024,8,64]{0,2,1:T(8,128)} %get-tuple-element.1063, f32[8,512,1024]{2,1,0:T(8,128)} %copy-done.1, f32[8,512,1024]{2,1,0:T(8,128)} %fusion.275, pred[]{:T(512)S(6)} %compare.6, bf16[1024,8,64]{0,2,1:T(8,128)(2,1)} %get-tuple-element.1084, s32[]{:T(128)S(6)} %select_n.103), kind=kOutput, calls=%fused_computation.44.clone.1 | convolution fusion | flops 558896128 | bytes 71827464 | tf_op jit(solution)/shard_map/while/body/eval_jaxpr/while/body/eval_jaxpr/hqk,qhd->khd/dot_general | solution.py:115
  475.8 8.1 fusion.275
  483.9 22.7 %fusion.276 = bf16[2,512,8,64]{1,3,2,0:T(8,128)(2,1)} fusion(bf16[2,512,8,64]{1,3,2,0:T(8,128)(2,1)} %get-tuple-element.1065, s32[]{:T(128)S(6)} %copy.136, bf16[1024,8,64]{0,2,1:T(8,128)(2,1)} %get-tuple-element.1087, f32[8,512,1024]{2,1,0:T(8,128)} %copy-done.1, f32[8,512,1024]{2,1,0:T(8,128)} %fusion.275), kind=kOutput, calls=%fused_computation.46.clone.1 | convolution fusion | flops 557847552 | bytes 69206016 | tf_op jit(solution)/shard_map/while/body/eval_jaxpr/while/body/eval_jaxpr/hqk,khd->qhd/dot_general | solution.py:112
  506.6 24.0 %bitcast_add_fusion.8 = f32[1024,8,64]{0,2,1:T(8,128)} fusion(f32[1024,8,64]{0,2,1:T(8,128)} %get-tuple-element.1063, f32[8,512,1024]{2,1,0:T(8,128)} %copy-done.1, f32[8,512,1024]{2,1,0:T(8,128)} %fusion.275, pred[]{:T(512)S(6)} %compare.6, bf16[1024,8,64]{0,2,1:T(8,128)(2,1)} %get-tuple-element.1084, s32[]{:T(128)S(6)} %select_n.103), kind=kOutput, calls=%fused_computation.44.clone.1 | convolution fusion | flops 558896128 | bytes 71827464 | tf_op jit(solution)/shard_map/while/body/eval_jaxpr/while/body/eval_jaxpr/hqk,qhd->khd/dot_general | solution.py:115
  549.7 142.0 %while.99 = (s32[]{:T(128)}, f32[1024,8,64]{0,2,1:T(8,128)}, f32[1024,8,64]{0,2,1:T(8,128)}, bf16[2,512,8,64]{1,3,2,0:T(8,128)(2,1)}, s32[2]{0:T(128)S(1)}, /*in...) while((s32[]{:T(128)}, f32[1024,8,64]{0,2,1:T(8,128)}, ...), condition=%wide.region_29.30_spmd.clone, body=%wide.region_27.29_spmd.clone.sunk | while | flops 2746755584 | bytes 267450688 | solution.py:127
  565.9 8.1 fusion.288
  574.1 22.7 %fusion.289 = bf16[2,512,8,64]{1,3,2,0:T(8,128)(2,1)} fusion(bf16[2,512,8,64]{1,3,2,0:T(8,128)(2,1)} %get-tuple-element.1115, s32[]{:T(128)S(6)} %copy.148, bf16[1024,8,64]{0,2,1:T(8,128)(2,1)} %get-tuple-element.1135, f32[8,512,1024]{2,1,0:T(8,128)} %copy-done.2, f32[8,512,1024]{2,1,0:T(8,128)} %fusion.288), kind=kOutput, calls=%fused_computation.78.clone.1 | convolution fusion | flops 557847552 | bytes 69206016 | tf_op jit(solution)/shard_map/while/body/eval_jaxpr/while/body/eval_jaxpr/hqk,khd->qhd/dot_general | solution.py:112
  596.7 23.4 %bitcast_add_fusion.10 = f32[1024,8,64]{0,2,1:T(8,128)} fusion(f32[1024,8,64]{0,2,1:T(8,128)} %get-tuple-element.1113, f32[8,512,1024]{2,1,0:T(8,128)} %copy-done.2, f32[8,512,1024]{2,1,0:T(8,128)} %fusion.288, pred[]{:T(512)S(6)} %compare.7, bf16[1024,8,64]{0,2,1:T(8,128)(2,1)} %get-tuple-element.1133, s32[]{:T(128)S(6)} %select_n.106), kind=kOutput, calls=%fused_computation.74.clone.1 | convolution fusion | flops 558896128 | bytes 71827464 | tf_op jit(solution)/shard_map/while/body/eval_jaxpr/while/body/eval_jaxpr/hqk,qhd->khd/dot_general | solution.py:115
  636.7 8.1 fusion.288
  644.8 22.7 %fusion.289 = bf16[2,512,8,64]{1,3,2,0:T(8,128)(2,1)} fusion(bf16[2,512,8,64]{1,3,2,0:T(8,128)(2,1)} %get-tuple-element.1115, s32[]{:T(128)S(6)} %copy.148, bf16[1024,8,64]{0,2,1:T(8,128)(2,1)} %get-tuple-element.1135, f32[8,512,1024]{2,1,0:T(8,128)} %copy-done.2, f32[8,512,1024]{2,1,0:T(8,128)} %fusion.288), kind=kOutput, calls=%fused_computation.78.clone.1 | convolution fusion | flops 557847552 | bytes 69206016 | tf_op jit(solution)/shard_map/while/body/eval_jaxpr/while/body/eval_jaxpr/hqk,khd->qhd/dot_general | solution.py:112
  667.5 24.0 %bitcast_add_fusion.10 = f32[1024,8,64]{0,2,1:T(8,128)} fusion(f32[1024,8,64]{0,2,1:T(8,128)} %get-tuple-element.1113, f32[8,512,1024]{2,1,0:T(8,128)} %copy-done.2, f32[8,512,1024]{2,1,0:T(8,128)} %fusion.288, pred[]{:T(512)S(6)} %compare.7, bf16[1024,8,64]{0,2,1:T(8,128)(2,1)} %get-tuple-element.1133, s32[]{:T(128)S(6)} %select_n.106), kind=kOutput, calls=%fused_computation.74.clone.1 | convolution fusion | flops 558896128 | bytes 71827464 | tf_op jit(solution)/shard_map/while/body/eval_jaxpr/while/body/eval_jaxpr/hqk,qhd->khd/dot_general | solution.py:115
  710.5 6.6 copy.90
  717.0 7.0 copy.103
  733.6 40.9 %all-reduce.5 = f32[3072]{0:T(1024)S(1)} all-reduce(f32[3072]{0:T(1024)S(1)} %reshape.670), channel_id=6, replica_groups=mesh['dp'=8,'shard'=4] {'dp','shard'}, use_global_device_ids=true, to_apply=%region_40.41.clone | all-reduce | flops 3072 | bytes 24576
  779.4 224.7 %all-reduce.9.cloned.1.call-done = (f32[1572864]{0:T(1024)}, f32[524288]{0:T(1024)}, f32[1048576]{0:T(1024)}, f32[1048576]{0:T(1024)}) async-done(((f32[1572864]{0:T(1024)}, f32[524288]{0:T(1024)}, f32[1048576]{0:T(1024)}, f32[1048576]{0:T(1024)}), (f32[1572864]{0:T(1024)}, f32[524288]{0:T(1024)}, f32[1048576]{0:T(1024)}, f32[1048576]{0:T(1024)})) %all-reduce.9.cloned.1.call-update) | async-done | bytes 16777232
  (389 shorter events, 272.1 us)
Async XLA Ops:
  7.2 254.9 %copy-start = (bf16[1,1024,512]{2,1,0:T(8,128)(2,1)S(1)}, bf16[1,1024,512]{2,1,0:T(8,128)(2,1)}, u32[]{:S(2)}) copy-start(bf16[1,1024,512]{2,1,0:T(8,128)(2,1)} %param.29) | copy-start | bytes 3145732
  7.2 55.6 %copy-start.51 = (bf16[1,1024,512]{2,1,0:T(8,128)(2,1)S(1)}, bf16[1,1024,512]{2,1,0:T(8,128)(2,1)}, u32[]{:S(2)}) copy-start(bf16[1,1024,512]{2,1,0:T(8,128)(2,1)} %param.28) | copy-start | bytes 3145732
  7.2 61.1 %all-gather.7.cloned.1.call-start = ((), (), s32[]{:S(2)}) async-start(), calls=%async_computation.1 | async-start | bytes 1081344 | tf_op jit(solution)/shard_map/all_gather | solution.py:187
  8.9 118.0 %all-gather.9.cloned.1.call-start = ((), (), s32[]{:S(2)}) async-start(), calls=%async_computation.2 | async-start | bytes 2162688 | tf_op jit(solution)/shard_map/all_gather | solution.py:191
  10.5 175.1 %all-gather.11.cloned.1.call-start = ((), (), s32[]{:S(2)}) async-start(), calls=%async_computation.3 | async-start | bytes 2162688 | tf_op jit(solution)/shard_map/all_gather | solution.py:192
  12.1 234.8 %all-gather.5.cloned.1.call-start = ((), (), s32[]{:S(2)}) async-start(), calls=%async_computation | async-start | bytes 3244032 | tf_op jit(solution)/shard_map/all_gather | solution.py:186
  13.8 990.4 %all-reduce.9.cloned.1.call-start = ((), (), s32[]{:S(2)}) async-start(), calls=%async_computation.4 | async-start | bytes 33554432
  398.8 6.4 copy-start.1
  468.8 6.9 copy-start.1
  559.6 6.4 copy-start.2
  629.8 6.9 copy-start.2
  696.6 6.3 copy-start.18
  697.2 9.8 copy-start.17
  699.3 9.4 copy-start.27
  731.7 42.7 %copy-start.96 = (f32[96]{0:T(128)S(1)}, f32[96]{0:T(128)}, u32[]{:S(2)}) copy-start(f32[96]{0:T(128)} %param.47) | copy-start | bytes 1156
  731.8 42.7 %copy-start.97 = (f32[96]{0:T(128)S(1)}, f32[96]{0:T(128)}, u32[]{:S(2)}) copy-start(f32[96]{0:T(128)} %param.46) | copy-start | bytes 1156
  733.6 43.6 %copy-start.28 = (bf16[1024,8,64]{0,2,1:T(8,128)(2,1)S(1)}, bf16[1024,8,64]{0,2,1:T(8,128)(2,1)}, u32[]{:S(2)}) copy-start(bf16[1024,8,64]{0,2,1:T(8,128)(2,1)} %copy-done.27) | copy-start | bytes 3145732
  733.6 43.7 %copy-start.48 = (bf16[512,512]{1,0:T(8,128)(2,1)S(1)}, bf16[512,512]{1,0:T(8,128)(2,1)}, u32[]{:S(2)}) copy-start(bf16[512,512]{1,0:T(8,128)(2,1)} %slice.171) | copy-start | bytes 1572868
  777.2 226.9 %copy-start.59 = (f32[49152]{0:T(1024)S(1)}, f32[49152]{0:T(1024)}, u32[]{:S(2)}) copy-start(f32[49152]{0:T(1024)} %param.35) | copy-start | bytes 589828
  777.3 226.9 %copy-start.60 = (f32[49152]{0:T(1024)S(1)}, f32[49152]{0:T(1024)}, u32[]{:S(2)}) copy-start(f32[49152]{0:T(1024)} %param.34) | copy-start | bytes 589828
  777.3 230.3 %copy-start.61 = (f32[32768]{0:T(1024)S(1)}, f32[32768]{0:T(1024)}, u32[]{:S(2)}) copy-start(f32[32768]{0:T(1024)} %param.41) | copy-start | bytes 393220
  777.3 230.3 %copy-start.62 = (f32[32768]{0:T(1024)S(1)}, f32[32768]{0:T(1024)}, u32[]{:S(2)}) copy-start(f32[32768]{0:T(1024)} %param.40) | copy-start | bytes 393220
  777.3 230.2 %copy-start.63 = (f32[32768]{0:T(1024)S(1)}, f32[32768]{0:T(1024)}, u32[]{:S(2)}) copy-start(f32[32768]{0:T(1024)} %param.44) | copy-start | bytes 393220
  777.3 230.2 %copy-start.64 = (f32[32768]{0:T(1024)S(1)}, f32[32768]{0:T(1024)}, u32[]{:S(2)}) copy-start(f32[32768]{0:T(1024)} %param.43) | copy-start | bytes 393220
  (85 other events, 202.6 us)
Sparse Core Ops, SparseCore 0:
  11.5 56.7 all-gather.6
  71.7 55.1 all-gather.8
  130.4 55.2 all-gather.10
  189.0 57.8 all-gather.4
  724.3 279.8 all-reduce.8
where the time goes:
time: 1030 us; the launch traced here: 1020 us
  waiting for transfers between devices  396 us (38%)
  matrix products  361 us (35%)
  local copies, waits for them, and re-layouts  91.7 us (9%)
  blocking collectives  83 us (8%)
  other arithmetic  46.3 us (4%)
  loops' own time  23.1 us (2%)
  between operations  15.5 us (2%)
    unnamed x6, waiting for transfers between devices  225 us
    dot_general x4, matrix products, one_block(): jnp.einsum('hqk,qhd->khd', grad_scores, q_block, preferred_element_type=j...  94.7 us
    dot_general x4, matrix products, one_block(): jnp.einsum('hqk,khd->qhd', grad_scores, k_row, preferred_element_type=jnp...  90.7 us
    unnamed x2, blocking collectives  83 us
    all_gather x1, waiting for transfers between devices, body(): lax.all_gather(inward_low, ('dp', 'shard'), axis=0, tiled=True)  56.9 us
    all_gather x1, waiting for transfers between devices, body(): lax.all_gather(expand_low, ('dp', 'shard'), axis=0, tiled=True)  55.1 us
    all_gather x1, waiting for transfers between devices, body(): lax.all_gather(shrink_low, ('dp', 'shard'), axis=0, tiled=True)  54.6 us
    dot_general x8, matrix products, one_block(): jnp.einsum('qhd,khd->hqk', q_block, k_row, preferred_element_type=jnp.flo...  39.5 us
  transfers between devices with their start and end apart: 5, of which 5 were waited for; matrix products, arithmetic and copies ran while one was open for 4% of the time, Pallas kernels for 0%

commit v1 on v0

--- a/solution.py
+++ b/solution.py
@@ -2,6 +2,7 @@
 import jax.numpy as jnp
 from jax import lax
 from jax.sharding import PartitionSpec as P
+from jax.lax import axis_index, axis_size, ppermute
 
 D = 512
 HEADS = 8
@@ -13,6 +14,25 @@
 learn_rate = 0.001
 beta_one = 0.9
 beta_two = 0.999
+
+
+def frames_reach(arr_in, axis_no):
+    row_out, e_next, r1 = (
+        axis_size(("dp", "shard")),
+        axis_index(("dp", "shard")),
+        arr_in.shape[axis_no],
+    )
+    arr_now, vec_out = (arr_in, 1)
+    while vec_out < row_out:
+        copies = []
+        for h in range(row_out):
+            copies.append((h, (h - vec_out) % row_out))
+        arr_now = jnp.concatenate(
+            [arr_now, ppermute(arr_now, axis_name=("dp", "shard"), perm=copies)], axis=axis_no
+        )
+        vec_out = 2 * vec_out
+    big = jnp.roll(arr_now, e_next * r1, axis=axis_no)
+    return big
 
 
 def matmul(left_mat, right_mat):
@@ -188,7 +208,7 @@
         lax.all_gather(norms_low, ("dp", "shard"), axis=0, tiled=True),
     )
     expand_all, shrink_all = (
-        lax.all_gather(expand_low, ("dp", "shard"), axis=0, tiled=True),
+        frames_reach(expand_low, 0),
         lax.all_gather(shrink_low, ("dp", "shard"), axis=0, tiled=True),
     )
     w_in, w_out, w_up, w_down, gains, biases = unpack(

time: 1030 us -> 1060 us (1.029)
  local copies, waits for them, and re-layouts: 91.7 us -> 110 us
  starting transfers between devices: 0.21 us -> 17.4 us
    ppermute x0 -> x5, waiting for transfers between devices: none -> 56 us  [frames_reach(): ppermute(arr_now, axis_name=('dp', 'shard'), perm=copies)]
    all_gather x1, waiting for transfers between devices: 54.6 us -> 10.2 us  [body(): lax.all_gather(shrink_low, ('dp', 'shard'), axis=0, tiled=True)]
    ppermute x0 -> x5, starting transfers between devices: none -> 17.2 us  [frames_reach(): ppermute(arr_now, axis_name=('dp', 'shard'), perm=copies)]
    unnamed x198 -> x216, local copies, waits for them, and re-layouts: 31.5 us -> 40.5 us
  transfers between devices with their start and end apart: 5 -> 10, of which waited for: 5 -> 8; matrix products, arithmetic and copies ran while one was open for 4% -> 5% of each run, Pallas kernels for 0% -> 0%
where the time goes in v1:
time: 1060 us; the launch traced here: 1050 us
  waiting for transfers between devices  403 us (38%)
  matrix products  361 us (34%)
  local copies, waits for them, and re-layouts  110 us (10%)
  blocking collectives  78 us (7%)
  other arithmetic  46.4 us (4%)
  loops' own time  23.1 us (2%)
  starting transfers between devices  17.4 us (2%)
  between operations  15.6 us (1%)
    unnamed x6, waiting for transfers between devices  225 us
    dot_general x4, matrix products, one_block(): jnp.einsum('hqk,qhd->khd', grad_scores, q_block, preferred_element_type=j...  94.5 us
    dot_general x4, matrix products, one_block(): jnp.einsum('hqk,khd->qhd', grad_scores, k_row, preferred_element_type=jnp...  90.7 us
    unnamed x2, blocking collectives  78 us
    all_gather x1, waiting for transfers between devices, body(): lax.all_gather(inward_low, ('dp', 'shard'), axis=0, tiled=True)  57.1 us
    ppermute x5, waiting for transfers between devices, frames_reach(): ppermute(arr_now, axis_name=('dp', 'shard'), perm=copies)  56 us
    all_gather x1, waiting for transfers between devices, body(): lax.all_gather(expand_low, ('dp', 'shard'), axis=0, tiled=True)  54.4 us
    unnamed x216, local copies, waits for them, and re-layouts  40.5 us
  transfers between devices with their start and end apart: 10, of which 8 were waited for; matrix products, arithmetic and copies ran while one was open for 5% of the time, Pallas kernels for 0%

profile of v1, /device:TPU:0, one launch (start us, length us, event | category | flops | bytes accessed | tf_op | source)
XLA Modules:
  0.0 1054.2 jit_solution(18210364870356924483)
XLA Ops:
  25.0 37.1 %all-reduce = bf16[3072]{0:T(1024)(128)(2,1)S(1)} all-reduce(bf16[3072]{0:T(1024)(128)(2,1)S(1)} %dynamic-update-slice), channel_id=1, replica_groups=mesh['dp'=8,'shard'=4] {'dp','shard'}, use_global_device_ids=true, to_apply=%add | all-reduce | flops 3072 | bytes 12288
  83.2 10.4 collective-permute-done.3
  104.2 40.2 %collective-permute-done.4 = bf16[524288]{0:T(1024)(128)(2,1)S(1)} collective-permute-done((bf16[524288]{0:T(1024)(128)(2,1)}, bf16[524288]{0:T(1024)(128)(2,1)S(1)}, u32[]{:S(2)}, u32[]{:S(2)}) %collective-permute-start.4) | collective-permute-done | bytes 1048608 | tf_op jit(solution)/shard_map/ppermute | solution.py:31
  154.0 10.2 all-gather.9.cloned.1.call-done
  168.5 54.4 %all-gather.11.cloned.1.call-done = bf16[1048576]{0:T(1024)(128)(2,1)} async-done(((bf16[32768]{0:T(1024)(128)(2,1)}), bf16[1048576]{0:T(1024)(128)(2,1)}) %all-gather.11.cloned.1.call-update) | async-done | bytes 2097168 | tf_op jit(solution)/shard_map/all_gather | solution.py:254
  227.0 57.1 %all-gather.5.cloned.1.call-done = bf16[1572864]{0:T(1024)(128)(2,1)} async-done(((bf16[49152]{0:T(1024)(128)(2,1)}), bf16[1572864]{0:T(1024)(128)(2,1)}) %all-gather.5.cloned.1.call-update) | async-done | bytes 3145744 | tf_op jit(solution)/shard_map/all_gather | solution.py:206
  304.2 33.5 %while.96 = (s32[]{:T(128)}, bf16[2,512,8,64]{1,3,2,0:T(8,128)(2,1)}, f32[2,8,512]{2,1,0:T(8,128)S(1)}, s32[2]{0:T(128)S(1)}, s32[1024]{0:T(1024)S(1)}, /*index=...) while((s32[]{:T(128)}, ...), condition=%wide.region_5.6_spmd, body=%wide.region_2.5_spmd.sunk | while | flops 1125642752 | bytes 64633092 | solution.py:100
  346.6 41.3 %while.97 = (s32[]{:T(128)}, bf16[2,512,8,64]{1,3,2,0:T(8,128)(2,1)}, f32[2,8,512]{2,1,0:T(8,128)S(1)}, s32[2]{0:T(128)S(1)}, s32[1024]{0:T(1024)S(1)}, /*index=...) while((s32[]{:T(128)}, ...), condition=%wide.region_13.14_spmd, body=%wide.region_10.13_spmd.sunk | while | flops 1124593664 | bytes 64628996 | solution.py:100
  426.3 141.6 %while.98 = (s32[]{:T(128)}, f32[1024,8,64]{0,2,1:T(8,128)}, f32[1024,8,64]{0,2,1:T(8,128)}, bf16[2,512,8,64]{1,3,2,0:T(8,128)(2,1)}, s32[2]{0:T(128)S(1)}, /*in...) while((s32[]{:T(128)}, f32[1024,8,64]{0,2,1:T(8,128)}, ...), condition=%wide.region_24.25_spmd.clone, body=%wide.region_22.24_spmd.clone.sunk | while | flops 2745706496 | bytes 267446608 | solution.py:147
  442.5 8.2 fusion.275
  450.6 22.7 %fusion.276 = bf16[2,512,8,64]{1,3,2,0:T(8,128)(2,1)} fusion(bf16[2,512,8,64]{1,3,2,0:T(8,128)(2,1)} %get-tuple-element.1075, s32[]{:T(128)S(6)} %copy.151, bf16[1024,8,64]{0,2,1:T(8,128)(2,1)} %get-tuple-element.1097, f32[8,512,1024]{2,1,0:T(8,128)} %copy-done.1, f32[8,512,1024]{2,1,0:T(8,128)} %fusion.275), kind=kOutput, calls=%fused_computation.46.clone.1 | convolution fusion | flops 557847552 | bytes 69206016 | tf_op jit(solution)/shard_map/while/body/eval_jaxpr/while/body/eval_jaxpr/hqk,khd->qhd/dot_general | solution.py:132
  473.3 23.3 %bitcast_add_fusion.8 = f32[1024,8,64]{0,2,1:T(8,128)} fusion(f32[1024,8,64]{0,2,1:T(8,128)} %get-tuple-element.1073, f32[8,512,1024]{2,1,0:T(8,128)} %copy-done.1, f32[8,512,1024]{2,1,0:T(8,128)} %fusion.275, pred[]{:T(512)S(6)} %compare.7, bf16[1024,8,64]{0,2,1:T(8,128)(2,1)} %get-tuple-element.1094, s32[]{:T(128)S(6)} %select_n.118), kind=kOutput, calls=%fused_computation.44.clone.1 | convolution fusion | flops 558896128 | bytes 71827464 | tf_op jit(solution)/shard_map/while/body/eval_jaxpr/while/body/eval_jaxpr/hqk,qhd->khd/dot_general | solution.py:135
  513.0 8.2 fusion.275
  521.2 22.7 %fusion.276 = bf16[2,512,8,64]{1,3,2,0:T(8,128)(2,1)} fusion(bf16[2,512,8,64]{1,3,2,0:T(8,128)(2,1)} %get-tuple-element.1075, s32[]{:T(128)S(6)} %copy.151, bf16[1024,8,64]{0,2,1:T(8,128)(2,1)} %get-tuple-element.1097, f32[8,512,1024]{2,1,0:T(8,128)} %copy-done.1, f32[8,512,1024]{2,1,0:T(8,128)} %fusion.275), kind=kOutput, calls=%fused_computation.46.clone.1 | convolution fusion | flops 557847552 | bytes 69206016 | tf_op jit(solution)/shard_map/while/body/eval_jaxpr/while/body/eval_jaxpr/hqk,khd->qhd/dot_general | solution.py:132
  543.8 23.9 %bitcast_add_fusion.8 = f32[1024,8,64]{0,2,1:T(8,128)} fusion(f32[1024,8,64]{0,2,1:T(8,128)} %get-tuple-element.1073, f32[8,512,1024]{2,1,0:T(8,128)} %copy-done.1, f32[8,512,1024]{2,1,0:T(8,128)} %fusion.275, pred[]{:T(512)S(6)} %compare.7, bf16[1024,8,64]{0,2,1:T(8,128)(2,1)} %get-tuple-element.1094, s32[]{:T(128)S(6)} %select_n.118), kind=kOutput, calls=%fused_computation.44.clone.1 | convolution fusion | flops 558896128 | bytes 71827464 | tf_op jit(solution)/shard_map/while/body/eval_jaxpr/while/body/eval_jaxpr/hqk,qhd->khd/dot_general | solution.py:135
  586.9 142.1 %while.99 = (s32[]{:T(128)}, f32[1024,8,64]{0,2,1:T(8,128)}, f32[1024,8,64]{0,2,1:T(8,128)}, bf16[2,512,8,64]{1,3,2,0:T(8,128)(2,1)}, s32[2]{0:T(128)S(1)}, /*in...) while((s32[]{:T(128)}, f32[1024,8,64]{0,2,1:T(8,128)}, ...), condition=%wide.region_29.30_spmd.clone, body=%wide.region_27.29_spmd.clone.sunk | while | flops 2746755584 | bytes 267450688 | solution.py:147
  603.2 8.2 fusion.288
  611.3 22.7 %fusion.289 = bf16[2,512,8,64]{1,3,2,0:T(8,128)(2,1)} fusion(bf16[2,512,8,64]{1,3,2,0:T(8,128)(2,1)} %get-tuple-element.1125, s32[]{:T(128)S(6)} %copy.163, bf16[1024,8,64]{0,2,1:T(8,128)(2,1)} %get-tuple-element.1145, f32[8,512,1024]{2,1,0:T(8,128)} %copy-done.2, f32[8,512,1024]{2,1,0:T(8,128)} %fusion.288), kind=kOutput, calls=%fused_computation.78.clone.1 | convolution fusion | flops 557847552 | bytes 69206016 | tf_op jit(solution)/shard_map/while/body/eval_jaxpr/while/body/eval_jaxpr/hqk,khd->qhd/dot_general | solution.py:132
  634.0 23.3 %bitcast_add_fusion.10 = f32[1024,8,64]{0,2,1:T(8,128)} fusion(f32[1024,8,64]{0,2,1:T(8,128)} %get-tuple-element.1123, f32[8,512,1024]{2,1,0:T(8,128)} %copy-done.2, f32[8,512,1024]{2,1,0:T(8,128)} %fusion.288, pred[]{:T(512)S(6)} %compare.8, bf16[1024,8,64]{0,2,1:T(8,128)(2,1)} %get-tuple-element.1143, s32[]{:T(128)S(6)} %select_n.121), kind=kOutput, calls=%fused_computation.74.clone.1 | convolution fusion | flops 558896128 | bytes 71827464 | tf_op jit(solution)/shard_map/while/body/eval_jaxpr/while/body/eval_jaxpr/hqk,qhd->khd/dot_general | solution.py:135
  674.0 8.2 fusion.288
  682.1 22.7 %fusion.289 = bf16[2,512,8,64]{1,3,2,0:T(8,128)(2,1)} fusion(bf16[2,512,8,64]{1,3,2,0:T(8,128)(2,1)} %get-tuple-element.1125, s32[]{:T(128)S(6)} %copy.163, bf16[1024,8,64]{0,2,1:T(8,128)(2,1)} %get-tuple-element.1145, f32[8,512,1024]{2,1,0:T(8,128)} %copy-done.2, f32[8,512,1024]{2,1,0:T(8,128)} %fusion.288), kind=kOutput, calls=%fused_computation.78.clone.1 | convolution fusion | flops 557847552 | bytes 69206016 | tf_op jit(solution)/shard_map/while/body/eval_jaxpr/while/body/eval_jaxpr/hqk,khd->qhd/dot_general | solution.py:132
  704.8 23.9 %bitcast_add_fusion.10 = f32[1024,8,64]{0,2,1:T(8,128)} fusion(f32[1024,8,64]{0,2,1:T(8,128)} %get-tuple-element.1123, f32[8,512,1024]{2,1,0:T(8,128)} %copy-done.2, f32[8,512,1024]{2,1,0:T(8,128)} %fusion.288, pred[]{:T(512)S(6)} %compare.8, bf16[1024,8,64]{0,2,1:T(8,128)(2,1)} %get-tuple-element.1143, s32[]{:T(128)S(6)} %select_n.121), kind=kOutput, calls=%fused_computation.74.clone.1 | convolution fusion | flops 558896128 | bytes 71827464 | tf_op jit(solution)/shard_map/while/body/eval_jaxpr/while/body/eval_jaxpr/hqk,qhd->khd/dot_general | solution.py:135
  771.0 40.9 %all-reduce.5 = f32[3072]{0:T(1024)S(1)} all-reduce(f32[3072]{0:T(1024)S(1)} %reshape.673), channel_id=6, replica_groups=mesh['dp'=8,'shard'=4] {'dp','shard'}, use_global_device_ids=true, to_apply=%region_40.41.clone | all-reduce | flops 3072 | bytes 24576
  816.8 225.0 %all-reduce.9.cloned.1.call-done = (f32[1572864]{0:T(1024)}, f32[524288]{0:T(1024)}, f32[1048576]{0:T(1024)}, f32[1048576]{0:T(1024)}) async-done(((f32[1572864]{0:T(1024)}, f32[524288]{0:T(1024)}, f32[1048576]{0:T(1024)}, f32[1048576]{0:T(1024)}), (f32[1572864]{0:T(1024)}, f32[524288]{0:T(1024)}, f32[1048576]{0:T(1024)}, f32[1048576]{0:T(1024)})) %all-reduce.9.cloned.1.call-update) | async-done | bytes 16777232
  (424 shorter events, 322.4 us)
Async XLA Ops:
  7.2 292.1 %copy-start = (bf16[1,1024,512]{2,1,0:T(8,128)(2,1)S(1)}, bf16[1,1024,512]{2,1,0:T(8,128)(2,1)}, u32[]{:S(2)}) copy-start(bf16[1,1024,512]{2,1,0:T(8,128)(2,1)} %param.29) | copy-start | bytes 3145732
  7.2 55.5 %copy-start.53 = (bf16[1,1024,512]{2,1,0:T(8,128)(2,1)S(1)}, bf16[1,1024,512]{2,1,0:T(8,128)(2,1)}, u32[]{:S(2)}) copy-start(bf16[1,1024,512]{2,1,0:T(8,128)(2,1)} %param.30) | copy-start | bytes 3145732
  7.2 90.4 %all-gather.7.cloned.1.call-start = ((), (), s32[]{:S(2)}) async-start(), calls=%async_computation.1 | async-start | bytes 1081344 | tf_op jit(solution)/shard_map/all_gather | solution.py:207
  8.9 155.3 %all-gather.9.cloned.1.call-start = ((), (), s32[]{:S(2)}) async-start(), calls=%async_computation.2 | async-start | bytes 2162688 | tf_op jit(solution)/shard_map/all_gather | solution.py:212
  10.5 212.4 %all-gather.11.cloned.1.call-start = ((), (), s32[]{:S(2)}) async-start(), calls=%async_computation.3 | async-start | bytes 2162688 | tf_op jit(solution)/shard_map/all_gather | solution.py:254
  12.1 272.0 %all-gather.5.cloned.1.call-start = ((), (), s32[]{:S(2)}) async-start(), calls=%async_computation | async-start | bytes 3244032 | tf_op jit(solution)/shard_map/all_gather | solution.py:206
  12.2 54.9 %collective-permute-start = (bf16[32768]{0:T(1024)(128)(2,1)}, bf16[32768]{0:T(1024)(128)(2,1)S(1)}, u32[]{:S(2)}, u32[]{:S(2)}) collective-permute-start(bf16[32768]{0:T(1024)(128)(2,1)} %get-tuple-element.683), channel_id=1, source_target_pairs={{0,31},{1,0},{2,1},{3,2},{4,3},{5,4},{6,5},{7,6},{8,7},{9,8},{10,9... | collective-permute-start | bytes 196616 | tf_op jit(solution)/shard_map/ppermute | solution.py:31
  20.2 1021.6 %all-reduce.9.cloned.1.call-start = ((), (), s32[]{:S(2)}) async-start(), calls=%async_computation.4 | async-start | bytes 33554432
  67.1 6.5 collective-permute-start.1
  73.6 6.4 collective-permute-start.2
  80.1 13.5 %collective-permute-start.3 = (bf16[262144]{0:T(1024)(128)(2,1)S(1)}, bf16[262144]{0:T(1024)(128)(2,1)S(1)}, u32[]{:S(2)}, u32[]{:S(2)}) collective-permute-start(bf16[262144]{0:T(1024)(128)(2,1)S(1)} %pad_maximum_fusion.1), channel_id=1, source_target_pairs={{0,24},{1,25},{2,26},{3,27},{4,28},{5,29},{6,30},{7,31},{8,0},{9,1... | collective-permute-start | bytes 1572872 | tf_op jit(solution)/shard_map/ppermute | solution.py:31
  95.5 49.0 %collective-permute-start.4 = (bf16[524288]{0:T(1024)(128)(2,1)}, bf16[524288]{0:T(1024)(128)(2,1)S(1)}, u32[]{:S(2)}, u32[]{:S(2)}) collective-permute-start(bf16[524288]{0:T(1024)(128)(2,1)} %copy-done.93), channel_id=1, source_target_pairs={{0,16},{1,17},{2,18},{3,19},{4,20},{5,21},{6,22},{7,23},{8,24},{9,... | collective-permute-start | bytes 3145736 | tf_op jit(solution)/shard_map/ppermute | solution.py:31
  734.5 9.8 copy-start.17
  736.6 9.4 copy-start.27
  769.1 42.8 %copy-start.100 = (f32[96]{0:T(128)S(1)}, f32[96]{0:T(128)}, u32[]{:S(2)}) copy-start(f32[96]{0:T(128)} %param.47) | copy-start | bytes 1156
  769.1 42.7 %copy-start.101 = (f32[96]{0:T(128)S(1)}, f32[96]{0:T(128)}, u32[]{:S(2)}) copy-start(f32[96]{0:T(128)} %param.46) | copy-start | bytes 1156
  771.0 43.7 %copy-start.28 = (bf16[1024,8,64]{0,2,1:T(8,128)(2,1)S(1)}, bf16[1024,8,64]{0,2,1:T(8,128)(2,1)}, u32[]{:S(2)}) copy-start(bf16[1024,8,64]{0,2,1:T(8,128)(2,1)} %copy-done.27) | copy-start | bytes 3145732
  771.0 43.7 %copy-start.50 = (bf16[512,512]{1,0:T(8,128)(2,1)S(1)}, bf16[512,512]{1,0:T(8,128)(2,1)}, u32[]{:S(2)}) copy-start(bf16[512,512]{1,0:T(8,128)(2,1)} %slice.171) | copy-start | bytes 1572868
  814.6 227.2 %copy-start.61 = (f32[49152]{0:T(1024)S(1)}, f32[49152]{0:T(1024)}, u32[]{:S(2)}) copy-start(f32[49152]{0:T(1024)} %param.35) | copy-start | bytes 589828
  814.6 227.2 %copy-start.62 = (f32[49152]{0:T(1024)S(1)}, f32[49152]{0:T(1024)}, u32[]{:S(2)}) copy-start(f32[49152]{0:T(1024)} %param.34) | copy-start | bytes 589828
  814.7 230.6 %copy-start.63 = (f32[32768]{0:T(1024)S(1)}, f32[32768]{0:T(1024)}, u32[]{:S(2)}) copy-start(f32[32768]{0:T(1024)} %param.41) | copy-start | bytes 393220
  814.7 230.5 %copy-start.64 = (f32[32768]{0:T(1024)S(1)}, f32[32768]{0:T(1024)}, u32[]{:S(2)}) copy-start(f32[32768]{0:T(1024)} %param.40) | copy-start | bytes 393220
  814.7 230.5 %copy-start.65 = (f32[32768]{0:T(1024)S(1)}, f32[32768]{0:T(1024)}, u32[]{:S(2)}) copy-start(f32[32768]{0:T(1024)} %param.44) | copy-start | bytes 393220
  814.7 230.5 %copy-start.66 = (f32[32768]{0:T(1024)S(1)}, f32[32768]{0:T(1024)}, u32[]{:S(2)}) copy-start(f32[32768]{0:T(1024)} %param.43) | copy-start | bytes 393220
  (94 other events, 251.7 us)
Sparse Core Ops, SparseCore 0:
  11.5 56.5 all-gather.6
  71.6 92.5 all-gather.8
  167.6 55.2 all-gather.10
  226.2 57.8 all-gather.4
  761.6 280.1 all-reduce.8
